TPU v7x, 32 devices: a whole 2x2x4 slice. The times are simulated.
32 devices in a mesh: seq: 8 (over z, core), expert: 4 (over y, x).
Axes of the slice: x: 2, y: 2, z: 4, core: 2. Of those that a mesh axis runs over, the one named last changes fastest.
Arguments:
- tokens: bfloat16 [4, 32, 4096], P('expert', 'seq'), may hold values from -6 to 6
- out_grad: bfloat16 [4, 32, 4096], P('expert', 'seq'), may hold values from -12 to 12
- expert_ids: int32 [4, 32, 8], P('expert', 'seq'), may hold values from 0 to 15, as said below
- route_gates: bfloat16 [4, 32, 8], P('expert', 'seq'), may hold values from 0.019897461 to 0.5
- gate_weight: bfloat16 [16, 1536, 4096], P('expert', 'seq'), may hold values from -0.09375 to 0.09375
- up_weight: bfloat16 [16, 1536, 4096], P('expert', 'seq'), may hold values from -0.09375 to 0.09375
- down_weight: bfloat16 [16, 1536, 4096], P('expert', 'seq'), may hold values from -0.15625 to 0.15625
Outputs:
- token_grad: bfloat16 [4, 32, 4096], P('expert', 'seq')
Inputs may be any that keep to these rules, and one draw needn't show every extreme that they name: `expert_ids`: each token names 8 different experts; within each index of the first dimension (one group of 32 tokens) every expert is named at most 32 times, and some expert exactly 32 times.
All inputs are finite; a program needn't handle non-finite values.
Results may differ from a plain program's by a relative error of at most 0.0057.
Values may be sent and summed in bfloat16 or wider, within the bound.
No kernel may reach another device: no remote copies, remote signals or barrier semaphores. Data moves between devices by JAX's collectives and lax.ppermute only.
A program may use at most 128 MiB of HBM per device.

v0:
```python
import jax
import jax.numpy as jnp
from jax import lax
from jax.sharding import PartitionSpec as P


def swiglu_back(gate_act, up_act, hidden_grad):
    sigmoid = jax.nn.sigmoid(gate_act)
    d_gate = (hidden_grad * up_act * sigmoid * (1.0 + gate_act * (1.0 - sigmoid))).astype(
        jnp.bfloat16
    )
    d_up = (hidden_grad * gate_act * sigmoid).astype(jnp.bfloat16)
    return (d_gate, d_up)


def expert_grads(input_rows, grad_rows, gate_rows, gate_mat, up_mat, down_mat):
    gate_act = jnp.einsum("ird,ifd->ifr", input_rows, gate_mat, preferred_element_type=jnp.float32)
    up_act = jnp.einsum("ird,ifd->ifr", input_rows, up_mat, preferred_element_type=jnp.float32)
    down_back = jnp.einsum("ird,ifd->ifr", grad_rows, down_mat, preferred_element_type=jnp.float32)
    hidden_grad = down_back * gate_rows.astype(jnp.float32)[:, None, :]
    d_gate, d_up = swiglu_back(gate_act, up_act, hidden_grad)
    summed = jnp.einsum("ifr,ifd->ird", d_gate, gate_mat, preferred_element_type=jnp.float32)
    summed = summed + jnp.einsum("ifr,ifd->ird", d_up, up_mat, preferred_element_type=jnp.float32)
    return summed.astype(jnp.bfloat16)


def per_device(tokens, out_grad, expert_ids, route_gates, gate_weight, up_weight, down_weight):
    gathered_x, gathered_dy, gathered_ids, gathered_gates = (
        lax.all_gather(tokens, "seq", axis=1, tiled=True),
        lax.all_gather(out_grad, "seq", axis=1, tiled=True),
        lax.all_gather(expert_ids, "seq", axis=1, tiled=True),
        lax.all_gather(route_gates, "seq", axis=1, tiled=True),
    )
    group_x = gathered_x[0]
    group_dy = gathered_dy[0]
    group_idx = gathered_ids[0]
    group_gates = gathered_gates[0]
    group_size, top_count = group_idx.shape
    model_width = group_x.shape[1]
    local_experts = gate_weight.shape[0]
    expert_peers = lax.axis_size("expert")
    seq_size = lax.axis_size("seq")
    experts = local_experts * expert_peers
    capacity = 2 * group_size * top_count // experts
    flat_ids = group_idx.reshape(-1)
    onehot = (flat_ids[:, None] == jnp.arange(experts, dtype=jnp.int32)[None, :]).astype(jnp.int32)
    position = jnp.sum(jnp.cumsum(onehot, axis=0) * onehot, axis=1) - 1
    slot_index = flat_ids * capacity + position
    route_token = jnp.arange(flat_ids.shape[0], dtype=jnp.int32) // top_count
    slot_token = (
        jnp.full((experts * capacity,), group_size, jnp.int32).at[slot_index].set(route_token)
    )
    slot_gate = (
        jnp.zeros((experts * capacity,), jnp.bfloat16).at[slot_index].set(group_gates.reshape(-1))
    )
    slot_owner = slot_token
    slot_token = slot_token.reshape(expert_peers, local_experts, capacity)
    slot_gate = slot_gate.reshape(expert_peers, local_experts, capacity)
    padded_x = jnp.concatenate([group_x, jnp.zeros((1, model_width), jnp.bfloat16)], axis=0)
    padded_dy = jnp.concatenate([group_dy, jnp.zeros((1, model_width), jnp.bfloat16)], axis=0)
    share_len = capacity // seq_size
    start_slot = lax.axis_index("seq") * share_len
    part_token = lax.dynamic_slice_in_dim(slot_token, start_slot, share_len, 2)
    part_gate = lax.dynamic_slice_in_dim(slot_gate, start_slot, share_len, 2)
    send_x = jnp.take(padded_x, part_token, axis=0)
    send_dy = jnp.take(padded_dy, part_token, axis=0)
    arrived_x, arrived_dy, arrived_gate = (
        lax.all_to_all(send_x, "expert", split_axis=0, concat_axis=2, tiled=True),
        lax.all_to_all(send_dy, "expert", split_axis=0, concat_axis=2, tiled=True),
        lax.all_to_all(part_gate, "expert", split_axis=0, concat_axis=2, tiled=True),
    )
    recv_x, recv_dy, recv_gate = (
        lax.all_gather(arrived_x, "seq", axis=2, tiled=True),
        lax.all_gather(arrived_dy, "seq", axis=2, tiled=True),
        lax.all_gather(arrived_gate, "seq", axis=2, tiled=True),
    )
    part_rows = expert_grads(
        recv_x[0], recv_dy[0], recv_gate[0], gate_weight, up_weight, down_weight
    )
    reshaped = part_rows.reshape(
        local_experts, seq_size, expert_peers, capacity // seq_size, model_width
    )
    returned = lax.all_to_all(reshaped, "expert", split_axis=2, concat_axis=0, tiled=True)
    flat_parts = returned.reshape(experts * capacity, model_width)
    wanted = jnp.arange(lax.axis_size("seq") * tokens.shape[1], dtype=jnp.int32)
    selector = (wanted[:, None] == slot_owner[None, :]).astype(jnp.bfloat16)
    summed = lax.psum_scatter(
        jnp.dot(selector, flat_parts, preferred_element_type=jnp.float32),
        "seq",
        scatter_dimension=0,
        tiled=True,
    )
    return summed.astype(jnp.bfloat16)[None]


def solution(mesh):
    in_specs = (
        P("expert", "seq", None),
        P("expert", "seq", None),
        P("expert", "seq", None),
        P("expert", "seq", None),
        P("expert", "seq", None),
        P("expert", "seq", None),
        P("expert", "seq", None),
    )
    out_specs = P("expert", "seq", None)
    return jax.shard_map(
        per_device, mesh=mesh, in_specs=in_specs, out_specs=out_specs, check_vma=False
    )
```

profile of v0, /device:TPU:0, one launch (start us, length us, event | category | flops | bytes accessed | tf_op | source)
XLA Modules:
  0.0 310.6 jit_solution(13137008721957007697)
XLA Ops:
  6.5 0.0 copy-start
  6.5 0.0 all-gather.5.cloned.1.call-start
  6.5 14.7 %all_gather.21 = s32[1,32,8]{2,0,1:T(1,128)S(1)} all-gather(s32[1,4,8]{2,0,1:T(1,128)} %bitcast.102), channel_id=1, replica_groups=mesh['seq'=8,'expert'=4] {'seq'}, dimensions={1}, use_global_device_ids=true | all-gather | bytes 1152 | tf_op jit(solution)/shard_map/all_gather | solution.py:31
  21.3 0.1 eq.43
  21.4 0.6 reduce-window.6
  22.0 0.2 slice_reduce_fusion
  22.2 0.5 broadcast.115
  22.7 0.7 fusion.50
  23.4 0.1 eq.39
  23.5 0.1 fusion.42
  23.6 0.1 mul.53
  23.7 1.4 scatter_custom_fusion
  25.1 0.1 reshape.77
  25.2 0.1 compare_and_fusion
  25.3 0.1 reshape.118
  25.4 0.8 copy.33
  26.2 14.9 %all_gather.22 = bf16[1,32,4096]{2,0,1:T(2,128)(2,1)S(1)} all-gather(bf16[1,4,4096]{2,0,1:T(2,128)(2,1)S(1)} %copy.33), channel_id=1, replica_groups=mesh['seq'=8,'expert'=4] {'seq'}, dimensions={1}, use_global_device_ids=true | all-gather | bytes 294912 | tf_op jit(solution)/shard_map/all_gather | solution.py:30
  41.1 0.3 copy.51
  41.4 0.9 gather_fusion
  42.3 0.2 reshape.121
  42.5 0.0 copy-done
  42.5 0.1 copy.39
  42.6 14.7 %all_gather.26 = bf16[1,32,4096]{2,0,1:T(2,128)(2,1)S(1)} all-gather(bf16[1,4,4096]{2,0,1:T(2,128)(2,1)S(1)} %copy.39), channel_id=1, replica_groups=mesh['seq'=8,'expert'=4] {'seq'}, dimensions={1}, use_global_device_ids=true | all-gather | bytes 294912 | tf_op jit(solution)/shard_map/all_gather | solution.py:29
  57.3 0.3 copy.50
  57.6 0.9 gather_fusion.1
  58.5 0.0 copy-start.1
  58.5 0.2 reshape.125
  58.7 0.6 broadcast_select_fusion
  59.3 12.5 %all_to_all.69 = bf16[4,4,4,4096]{3,2,1,0:T(4,128)(2,1)S(1)} all-to-all(bf16[4,4,4,4096]{3,2,1,0:T(4,128)(2,1)S(1)} %get-tuple-element.10), channel_id=1, replica_groups=mesh['seq'=8,'expert'=4] {'expert'}, dimensions={0} | all-to-all | bytes 1048576 | tf_op jit(solution)/shard_map/all_to_all | solution.py:68
  71.8 0.2 copy.40
  72.0 0.9 all_to_all.61
  72.9 0.0 all-gather.5.cloned.1.call-update
  72.9 0.0 all-gather.3.cloned.1.call-start
  73.0 10.2 %all_to_all.70 = bf16[4,4,4,4096]{3,2,1,0:T(4,128)(2,1)S(1)} all-to-all(bf16[4,4,4,4096]{3,2,1,0:T(4,128)(2,1)S(1)} %get-tuple-element.11), channel_id=1, replica_groups=mesh['seq'=8,'expert'=4] {'expert'}, dimensions={0} | all-to-all | bytes 1048576 | tf_op jit(solution)/shard_map/all_to_all | solution.py:69
  83.2 0.2 copy.34
  83.4 0.9 all_to_all.53
  84.4 0.0 all-gather.3.cloned.1.call-update
  84.4 0.0 copy-done.1
  84.4 13.4 %all_gather.24 = bf16[1,32,8]{2,0,1:T(2,128)(2,1)S(1)} all-gather(bf16[1,4,8]{2,0,1:T(2,128)(2,1)S(1)} %copy.35), channel_id=1, replica_groups=mesh['seq'=8,'expert'=4] {'seq'}, dimensions={1}, use_global_device_ids=true | all-gather | bytes 576 | tf_op jit(solution)/shard_map/all_gather | solution.py:32
  97.9 0.1 reduce.4
  97.9 0.1 reshape.110
  98.0 2.2 scatter_custom_fusion.1
  100.2 0.1 reshape.78
  100.3 0.1 constant_dynamic-slice_fusion
  100.3 7.0 %all_to_all.71 = bf16[4,4,4]{2,1,0:T(4,128)(2,1)S(1)} all-to-all(bf16[4,4,4]{2,1,0:T(4,128)(2,1)S(1)} %constant_dynamic-slice_fusion), channel_id=1, replica_groups=mesh['seq'=8,'expert'=4] {'expert'}, dimensions={0} | all-to-all | bytes 256 | tf_op jit(solution)/shard_map/all_to_all | solution.py:70
  107.4 0.1 copy.42
  107.5 14.3 %all_gather.25 = bf16[1,4,128]{1,0,2:T(2,128)(2,1)S(1)} all-gather(bf16[1,4,16]{1,0,2:T(2,128)(2,1)S(1)} %reshape.126), channel_id=1, replica_groups=mesh['seq'=8,'expert'=4] {'seq'}, dimensions={2}, use_global_device_ids=true | all-gather | bytes 1152 | tf_op jit(solution)/shard_map/all_gather | solution.py:75
  121.8 0.1 convert_element_type.35
  121.9 0.1 copy.38
  121.9 5.9 %fusion.9 = f32[4,192,128]{2,1,0:T(8,128)S(1)} fusion(bf16[4,192,4096]{2,1,0:T(8,128)(2,1)} %param.13, bf16[1,4,128,4096]{3,2,1,0:T(8,128)(2,1)} %all-gather.5.cloned.1.call-done), kind=kOutput, calls=%fused_computation.12 | convolution fusion | flops 805306368 | bytes 10878976 | tf_op jit(solution)/shard_map/ird,ifd->ifr/dot_general | solution.py:17
  127.9 38.2 %all-gather.3.cloned.1.call-done = bf16[1,4,128,4096]{3,2,1,0:T(8,128)(2,1)} async-done(((bf16[1,4,16,4096]{3,2,1,0:T(8,128)(2,1)}), bf16[1,4,128,4096]{3,2,1,0:T(8,128)(2,1)}) %all-gather.3.cloned.1.call-update) | async-done | bytes 4194320 | tf_op jit(solution)/shard_map/all_gather | solution.py:74
  166.1 5.8 %fusion.24 = f32[4,192,128]{2,1,0:T(8,128)S(1)} fusion(bf16[4,192,4096]{2,1,0:T(8,128)(2,1)} %param.15, bf16[1,4,128,4096]{3,2,1,0:T(8,128)(2,1)} %all-gather.3.cloned.1.call-done, f32[4,128]{1,0:T(4,128)S(1)} %copy.38), kind=kOutput, calls=%fused_computation.17 | convolution fusion | flops 805404672 | bytes 10881024 | tf_op jit(solution)/shard_map/ird,ifd->ifr/dot_general | solution.py:19
  171.9 11.9 %fusion.31 = f32[4,128,4096]{2,1,0:T(8,128)} fusion(bf16[4,192,4096]{2,1,0:T(8,128)(2,1)} %param.13, f32[4,192,128]{2,1,0:T(8,128)S(1)} %fusion.24, bf16[4,192,4096]{2,1,0:T(8,128)(2,1)} %param.14, bf16[1,4,128,4096]{3,2,1,0:T(8,128)(2,1)} %all-gather.5.cloned.1.call-done, f32[4,192,128]{2,1,0:T(8,128)S(1)} %fusion.9), kind=kOutput, calls=%fused_computation.19 | convolution fusion | flops 1611595776 | bytes 25952256 | tf_op jit(solution)/shard_map/ifr,ifd->ird/dot_general | solution.py:22
  183.8 8.5 %add_convert_fusion = bf16[4,128,4096]{2,1,0:T(8,128)(2,1)} fusion(f32[4,128,4096]{2,1,0:T(8,128)} %fusion.31, bf16[4,192,4096]{2,1,0:T(8,128)(2,1)} %param.14, f32[4,192,128]{2,1,0:T(8,128)S(1)} %fusion.24, f32[4,192,128]{2,1,0:T(8,128)S(1)} %fusion.9), kind=kOutput, calls=%fused_computation.4 | convolution fusion | flops 810090496 | bytes 19660800 | tf_op jit(solution)/shard_map/ifr,ifd->ird/dot_general | solution.py:23
  192.4 7.2 %reshape.79 = bf16[4,8,4,4,4096]{4,3,2,1,0:T(4,128)(2,1)} reshape(bf16[4,128,4096]{2,1,0:T(8,128)(2,1)} %add_convert_fusion) | data formatting | bytes 8388608 | tf_op jit(solution)/shard_map/reshape | solution.py:80
  199.6 7.9 %copy.41 = bf16[4,8,4,4,4096]{4,3,1,0,2:T(4,128)(2,1)} copy(bf16[4,8,4,4,4096]{4,3,2,1,0:T(4,128)(2,1)} %reshape.79) | data formatting | bytes 8388608 | tf_op jit(solution)/shard_map/reshape | solution.py:80
  207.4 5.0 %all-to-all-start.3 = ((bf16[4,8,4,4,4096]{4,3,1,0,2:T(4,128)(2,1)}), bf16[4,8,4,4,4096]{4,3,1,0,2:T(4,128)(2,1)}, u32[]{:S(2)}, u32[]{:S(2)}) async-start(bf16[4,8,4,4,4096]{4,3,1,0,2:T(4,128)(2,1)} %copy.41), calls=%async_computation.3 | async-start | bytes 8388608 | tf_op jit(solution)/shard_map/all_to_all | solution.py:83
  212.4 0.0 copy-done.2
  212.5 0.6 dynamic-slice
  213.7 46.8 %all-to-all-done.3 = bf16[4,8,4,4,4096]{4,3,1,0,2:T(4,128)(2,1)} async-done(((bf16[4,8,4,4,4096]{4,3,1,0,2:T(4,128)(2,1)}), bf16[4,8,4,4,4096]{4,3,1,0,2:T(4,128)(2,1)}, u32[]{:S(2)}, u32[]{:S(2)}) %all-to-all-start.3) | async-done | bytes 4194336 | tf_op jit(solution)/shard_map/all_to_all | solution.py:83
  260.5 6.9 %reshape.80 = bf16[512,4096]{1,0:T(8,128)(2,1)} reshape(bf16[4,4,8,1,4,4096]{5,4,2,1,0,3:T(4,128)(2,1)} %bitcast.17) | data formatting | bytes 8388608 | tf_op jit(solution)/shard_map/reshape | solution.py:84
  267.4 3.0 fusion.38
  270.4 32.7 %all-reduce.4 = bf16[32,4096]{1,0:T(8,128)(2,1)S(1)} all-reduce(f32[32,4096]{1,0:T(8,128)S(1)} %fusion.38), channel_id=2, replica_groups=mesh['seq'=8,'expert'=4] {'seq'}, use_global_device_ids=true, to_apply=%region_5.7.clone | all-reduce | flops 131072 | bytes 786432
  303.1 0.6 fusion.39
  (13 shorter events, 0.1 us)
Async XLA Ops:
  6.5 36.0 %copy-start = (bf16[1,4,4096]{2,1,0:T(4,128)(2,1)S(1)}, bf16[1,4,4096]{2,1,0:T(4,128)(2,1)}, u32[]{:S(2)}) copy-start(bf16[1,4,4096]{2,1,0:T(4,128)(2,1)} %param.9) | copy-start | bytes 98308
  6.5 115.4 %all-gather.5.cloned.1.call-start = ((), (), s32[]{:S(2)}) async-start(), calls=%async_computation.5 | async-start | bytes 4718592 | tf_op jit(solution)/shard_map/all_gather | solution.py:73
  58.5 25.9 %copy-start.1 = (bf16[1,4,8]{2,1,0:T(4,128)(2,1)S(1)}, bf16[1,4,8]{2,1,0:T(4,128)(2,1)}, u32[]{:S(2)}) copy-start(bf16[1,4,8]{2,1,0:T(4,128)(2,1)} %param.12) | copy-start | bytes 196
  72.9 93.1 %all-gather.3.cloned.1.call-start = ((), (), s32[]{:S(2)}) async-start(), calls=%async_computation.4 | async-start | bytes 4718592 | tf_op jit(solution)/shard_map/all_gather | solution.py:74
  207.4 5.0 %copy-start.2 = (u32[32]{0:T(128)S(1)}, u32[32]{0:T(128)}, u32[]{:S(2)}) copy-start(u32[32]{0:T(128)} %constant.65) | copy-start | bytes 388
  207.4 53.1 %all-to-all-start.3 = ((bf16[4,8,4,4,4096]{4,3,1,0,2:T(4,128)(2,1)}), bf16[4,8,4,4,4096]{4,3,1,0,2:T(4,128)(2,1)}, u32[]{:S(2)}, u32[]{:S(2)}) async-start(bf16[4,8,4,4,4096]{4,3,1,0,2:T(4,128)(2,1)} %copy.41), calls=%async_computation.3 | async-start | bytes 8388608 | tf_op jit(solution)/shard_map/all_to_all | solution.py:83
Sparse Core Ops, SparseCore 0:
  73.1 45.5 all-gather.4
  120.3 45.7 all-gather.2
where the time goes:
time: 311 us
  blocking collectives  134 us (43%)
  waiting for transfers between devices  85.1 us (27%)
  matrix products  35.2 us (11%)
  local copies, waits for them, and re-layouts  34.2 us (11%)
  between operations  14.3 us (5%)
  starting transfers between devices  5.03 us (2%)
    all_to_all x1, waiting for transfers between devices, per_device(): lax.all_to_all(reshaped, 'expert', split_axis=2, concat_axis=0, tiled=True)  46.8 us
    all_gather x1, waiting for transfers between devices, per_device(): lax.all_gather(arrived_dy, 'seq', axis=2, tiled=True)  38.2 us
    unnamed x1, blocking collectives  32.7 us
    reshape x2, local copies, waits for them, and re-layouts, per_device(): part_rows.reshape(local_experts, seq_size, expert_peers, capacity // seq_...  15.1 us
    all_gather x1, blocking collectives, per_device(): lax.all_gather(out_grad, 'seq', axis=1, tiled=True)  14.9 us
    all_gather x1, blocking collectives, per_device(): lax.all_gather(expert_ids, 'seq', axis=1, tiled=True)  14.7 us
    all_gather x1, blocking collectives, per_device(): lax.all_gather(tokens, 'seq', axis=1, tiled=True)  14.7 us
    all_gather x1, blocking collectives, per_device(): lax.all_gather(arrived_gate, 'seq', axis=2, tiled=True)  14.3 us
  transfers between devices with their start and end apart: 3, of which 2 were waited for; matrix products, arithmetic and copies ran while one was open for 3% of the time, Pallas kernels for 0%

commit v1 on v0

--- a/solution.py
+++ b/solution.py
@@ -2,6 +2,14 @@
 import jax.numpy as jnp
 from jax import lax
 from jax.sharding import PartitionSpec as P
+
+
+def tiled_gather(shard, axis, dim):
+    devices = lax.axis_size(axis)
+    repeats = [devices if d == dim else 1 for d in range(shard.ndim)]
+    return lax.all_to_all(
+        jnp.tile(shard, repeats), axis, split_axis=dim, concat_axis=dim, tiled=True
+    )
 
 
 def swiglu_back(gate_act, up_act, hidden_grad):
@@ -28,7 +36,7 @@
     gathered_x, gathered_dy, gathered_ids, gathered_gates = (
         lax.all_gather(tokens, "seq", axis=1, tiled=True),
         lax.all_gather(out_grad, "seq", axis=1, tiled=True),
-        lax.all_gather(expert_ids, "seq", axis=1, tiled=True),
+        tiled_gather(expert_ids, "seq", 1),
         lax.all_gather(route_gates, "seq", axis=1, tiled=True),
     )
     group_x = gathered_x[0]

time: 311 us -> 307 us (0.987)
  blocking collectives: 134 us -> 120 us
  starting transfers between devices: 5.03 us -> 11.4 us
    all_gather x1 -> x0, blocking collectives: 14.7 us -> none  [per_device(): lax.all_gather(expert_ids, 'seq', axis=1, tiled=True)]
    all_to_all x0 -> x1, starting transfers between devices: none -> 6.35 us  [tiled_gather(): lax.all_to_all(jnp.tile(shard, repeats), axis, split_axis=dim, concat_axi...]
  transfers between devices with their start and end apart: 3 -> 4, of which waited for: 2 -> 2; matrix products, arithmetic and copies ran while one was open for 3% -> 4% of each run, Pallas kernels for 0% -> 0%
where the time goes in v1:
time: 307 us; the launch traced here: 306 us
  blocking collectives  120 us (39%)
  waiting for transfers between devices  86.7 us (28%)
  local copies, waits for them, and re-layouts  36.3 us (12%)
  matrix products  35.1 us (11%)
  between operations  14.3 us (5%)
  starting transfers between devices  11.4 us (4%)
    all_to_all x1, waiting for transfers between devices, per_device(): lax.all_to_all(reshaped, 'expert', split_axis=2, concat_axis=0, tiled=True)  46.8 us
    all_gather x1, waiting for transfers between devices, per_device(): lax.all_gather(arrived_dy, 'seq', axis=2, tiled=True)  39.8 us
    unnamed x1, blocking collectives  32.7 us
    all_gather x1, blocking collectives, per_device(): lax.all_gather(out_grad, 'seq', axis=1, tiled=True)  15.2 us
    reshape x2, local copies, waits for them, and re-layouts, per_device(): part_rows.reshape(local_experts, seq_size, expert_peers, capacity // seq_...  15.1 us
    all_gather x1, blocking collectives, per_device(): lax.all_gather(tokens, 'seq', axis=1, tiled=True)  14.8 us
    all_gather x1, blocking collectives, per_device(): lax.all_gather(arrived_gate, 'seq', axis=2, tiled=True)  14.6 us
    all_gather x1, blocking collectives, per_device(): lax.all_gather(route_gates, 'seq', axis=1, tiled=True)  13.4 us
  transfers between devices with their start and end apart: 4, of which 2 were waited for; matrix products, arithmetic and copies ran while one was open for 4% of the time, Pallas kernels for 0%

profile of v1, /device:TPU:0, one launch (start us, length us, event | category | flops | bytes accessed | tf_op | source)
XLA Modules:
  0.0 306.3 jit_solution(13285103180171934944)
XLA Ops:
  6.5 1.3 tile.12
  7.8 6.4 %all-to-all-start = ((s32[1,32,8]{2,0,1:T(1,128)}), s32[1,32,8]{2,0,1:T(1,128)S(1)}, u32[]{:S(2)}, u32[]{:S(2)}) async-start(s32[1,32,8]{2,0,1:T(1,128)} %bitcast.1), calls=%async_computation | async-start | bytes 32768 | tf_op jit(solution)/shard_map/all_to_all | solution.py:10
  14.2 0.0 all-gather.5.cloned.1.call-start
  14.2 0.8 copy.31
  15.0 15.2 %all_gather.18 = bf16[1,32,4096]{2,0,1:T(2,128)(2,1)S(1)} all-gather(bf16[1,4,4096]{2,0,1:T(2,128)(2,1)S(1)} %copy.31), channel_id=1, replica_groups=mesh['seq'=8,'expert'=4] {'seq'}, dimensions={1}, use_global_device_ids=true | all-gather | bytes 294912 | tf_op jit(solution)/shard_map/all_gather | solution.py:38
  30.2 0.8 copy.37
  31.0 14.8 %all_gather.22 = bf16[1,32,4096]{2,0,1:T(2,128)(2,1)S(1)} all-gather(bf16[1,4,4096]{2,0,1:T(2,128)(2,1)S(1)} %copy.37), channel_id=1, replica_groups=mesh['seq'=8,'expert'=4] {'seq'}, dimensions={1}, use_global_device_ids=true | all-gather | bytes 294912 | tf_op jit(solution)/shard_map/all_gather | solution.py:37
  45.8 0.3 copy.49
  46.1 0.3 copy.48
  46.5 0.0 all-to-all-done
  46.5 0.1 eq.43
  46.6 0.6 reduce-window.6
  47.2 0.2 slice_reduce_fusion
  47.4 0.5 broadcast.118
  47.9 0.7 fusion.50
  48.7 0.1 eq.39
  48.7 0.1 fusion.42
  48.8 0.1 mul.53
  48.9 1.4 scatter_custom_fusion
  50.3 0.1 reshape.83
  50.4 0.1 compare_and_fusion
  50.5 0.1 reshape.124
  50.6 0.9 gather_fusion
  51.5 0.2 reshape.127
  51.7 0.9 gather_fusion.1
  52.6 0.0 copy-start
  52.6 0.2 reshape.131
  52.8 0.6 broadcast_select_fusion
  53.3 12.5 %all_to_all.74 = bf16[4,4,4,4096]{3,2,1,0:T(4,128)(2,1)S(1)} all-to-all(bf16[4,4,4,4096]{3,2,1,0:T(4,128)(2,1)S(1)} %get-tuple-element.10), channel_id=1, replica_groups=mesh['seq'=8,'expert'=4] {'expert'}, dimensions={0} | all-to-all | bytes 1048576 | tf_op jit(solution)/shard_map/all_to_all | solution.py:76
  65.9 0.2 copy.38
  66.1 0.9 all_to_all.65
  67.0 0.0 all-gather.5.cloned.1.call-update
  67.0 0.0 all-gather.3.cloned.1.call-start
  67.1 10.2 %all_to_all.75 = bf16[4,4,4,4096]{3,2,1,0:T(4,128)(2,1)S(1)} all-to-all(bf16[4,4,4,4096]{3,2,1,0:T(4,128)(2,1)S(1)} %get-tuple-element.11), channel_id=1, replica_groups=mesh['seq'=8,'expert'=4] {'expert'}, dimensions={0} | all-to-all | bytes 1048576 | tf_op jit(solution)/shard_map/all_to_all | solution.py:77
  77.3 0.2 copy.32
  77.5 0.9 all_to_all.57
  78.5 0.0 all-gather.3.cloned.1.call-update
  78.5 0.0 copy-done
  78.5 13.4 %all_gather.20 = bf16[1,32,8]{2,0,1:T(2,128)(2,1)S(1)} all-gather(bf16[1,4,8]{2,0,1:T(2,128)(2,1)S(1)} %copy.33), channel_id=1, replica_groups=mesh['seq'=8,'expert'=4] {'seq'}, dimensions={1}, use_global_device_ids=true | all-gather | bytes 576 | tf_op jit(solution)/shard_map/all_gather | solution.py:40
  91.9 0.1 reduce.4
  91.9 0.1 reshape.116
  92.0 2.2 scatter_custom_fusion.1
  94.2 0.1 reshape.84
  94.3 0.1 constant_dynamic-slice_fusion
  94.4 7.0 %all_to_all.76 = bf16[4,4,4]{2,1,0:T(4,128)(2,1)S(1)} all-to-all(bf16[4,4,4]{2,1,0:T(4,128)(2,1)S(1)} %constant_dynamic-slice_fusion), channel_id=1, replica_groups=mesh['seq'=8,'expert'=4] {'expert'}, dimensions={0} | all-to-all | bytes 256 | tf_op jit(solution)/shard_map/all_to_all | solution.py:78
  101.4 0.1 copy.40
  101.5 14.6 %all_gather.21 = bf16[1,4,128]{1,0,2:T(2,128)(2,1)S(1)} all-gather(bf16[1,4,16]{1,0,2:T(2,128)(2,1)S(1)} %reshape.132), channel_id=1, replica_groups=mesh['seq'=8,'expert'=4] {'seq'}, dimensions={2}, use_global_device_ids=true | all-gather | bytes 1152 | tf_op jit(solution)/shard_map/all_gather | solution.py:83
  116.1 0.1 convert_element_type.35
  116.2 0.1 copy.36
  116.2 5.9 %fusion.9 = f32[4,192,128]{2,1,0:T(8,128)S(1)} fusion(bf16[4,192,4096]{2,1,0:T(8,128)(2,1)} %param.13, bf16[1,4,128,4096]{3,2,1,0:T(8,128)(2,1)} %all-gather.5.cloned.1.call-done), kind=kOutput, calls=%fused_computation.12 | convolution fusion | flops 805306368 | bytes 10878976 | tf_op jit(solution)/shard_map/ird,ifd->ifr/dot_general | solution.py:25
  122.1 39.8 %all-gather.3.cloned.1.call-done = bf16[1,4,128,4096]{3,2,1,0:T(8,128)(2,1)} async-done(((bf16[1,4,16,4096]{3,2,1,0:T(8,128)(2,1)}), bf16[1,4,128,4096]{3,2,1,0:T(8,128)(2,1)}) %all-gather.3.cloned.1.call-update) | async-done | bytes 4194320 | tf_op jit(solution)/shard_map/all_gather | solution.py:82
  161.9 5.8 %fusion.24 = f32[4,192,128]{2,1,0:T(8,128)S(1)} fusion(bf16[4,192,4096]{2,1,0:T(8,128)(2,1)} %param.15, bf16[1,4,128,4096]{3,2,1,0:T(8,128)(2,1)} %all-gather.3.cloned.1.call-done, f32[4,128]{1,0:T(4,128)S(1)} %copy.36), kind=kOutput, calls=%fused_computation.17 | convolution fusion | flops 805404672 | bytes 10881024 | tf_op jit(solution)/shard_map/ird,ifd->ifr/dot_general | solution.py:27
  167.7 11.9 %fusion.31 = f32[4,128,4096]{2,1,0:T(8,128)} fusion(bf16[4,192,4096]{2,1,0:T(8,128)(2,1)} %param.13, f32[4,192,128]{2,1,0:T(8,128)S(1)} %fusion.24, bf16[4,192,4096]{2,1,0:T(8,128)(2,1)} %param.14, bf16[1,4,128,4096]{3,2,1,0:T(8,128)(2,1)} %all-gather.5.cloned.1.call-done, f32[4,192,128]{2,1,0:T(8,128)S(1)} %fusion.9), kind=kOutput, calls=%fused_computation.19 | convolution fusion | flops 1611595776 | bytes 25952256 | tf_op jit(solution)/shard_map/ifr,ifd->ird/dot_general | solution.py:30
  179.6 8.5 %add_convert_fusion = bf16[4,128,4096]{2,1,0:T(8,128)(2,1)} fusion(f32[4,128,4096]{2,1,0:T(8,128)} %fusion.31, bf16[4,192,4096]{2,1,0:T(8,128)(2,1)} %param.14, f32[4,192,128]{2,1,0:T(8,128)S(1)} %fusion.24, f32[4,192,128]{2,1,0:T(8,128)S(1)} %fusion.9), kind=kOutput, calls=%fused_computation.4 | convolution fusion | flops 810090496 | bytes 19660800 | tf_op jit(solution)/shard_map/ifr,ifd->ird/dot_general | solution.py:31
  188.2 7.2 %reshape.85 = bf16[4,8,4,4,4096]{4,3,2,1,0:T(4,128)(2,1)} reshape(bf16[4,128,4096]{2,1,0:T(8,128)(2,1)} %add_convert_fusion) | data formatting | bytes 8388608 | tf_op jit(solution)/shard_map/reshape | solution.py:88
  195.4 7.9 %copy.39 = bf16[4,8,4,4,4096]{4,3,1,0,2:T(4,128)(2,1)} copy(bf16[4,8,4,4,4096]{4,3,2,1,0:T(4,128)(2,1)} %reshape.85) | data formatting | bytes 8388608 | tf_op jit(solution)/shard_map/reshape | solution.py:88
  203.2 5.0 %all-to-all-start.4 = ((bf16[4,8,4,4,4096]{4,3,1,0,2:T(4,128)(2,1)}), bf16[4,8,4,4,4096]{4,3,1,0,2:T(4,128)(2,1)}, u32[]{:S(2)}, u32[]{:S(2)}) async-start(bf16[4,8,4,4,4096]{4,3,1,0,2:T(4,128)(2,1)} %copy.39), calls=%async_computation.4 | async-start | bytes 8388608 | tf_op jit(solution)/shard_map/all_to_all | solution.py:91
  208.2 0.0 copy-done.1
  208.2 0.6 dynamic-slice
  209.5 46.8 %all-to-all-done.4 = bf16[4,8,4,4,4096]{4,3,1,0,2:T(4,128)(2,1)} async-done(((bf16[4,8,4,4,4096]{4,3,1,0,2:T(4,128)(2,1)}), bf16[4,8,4,4,4096]{4,3,1,0,2:T(4,128)(2,1)}, u32[]{:S(2)}, u32[]{:S(2)}) %all-to-all-start.4) | async-done | bytes 4194336 | tf_op jit(solution)/shard_map/all_to_all | solution.py:91
  256.3 6.9 %reshape.86 = bf16[512,4096]{1,0:T(8,128)(2,1)} reshape(bf16[4,4,8,1,4,4096]{5,4,2,1,0,3:T(4,128)(2,1)} %bitcast.18) | data formatting | bytes 8388608 | tf_op jit(solution)/shard_map/reshape | solution.py:92
  263.2 3.0 fusion.38
  266.2 32.7 %all-reduce.4 = bf16[32,4096]{1,0:T(8,128)(2,1)S(1)} all-reduce(f32[32,4096]{1,0:T(8,128)S(1)} %fusion.38), channel_id=2, replica_groups=mesh['seq'=8,'expert'=4] {'seq'}, use_global_device_ids=true, to_apply=%region_5.7.clone | all-reduce | flops 131072 | bytes 786432
  298.9 0.6 fusion.39
  (13 shorter events, 0.1 us)
Async XLA Ops:
  7.8 38.7 %all-to-all-start = ((s32[1,32,8]{2,0,1:T(1,128)}), s32[1,32,8]{2,0,1:T(1,128)S(1)}, u32[]{:S(2)}, u32[]{:S(2)}) async-start(s32[1,32,8]{2,0,1:T(1,128)} %bitcast.1), calls=%async_computation | async-start | bytes 32768 | tf_op jit(solution)/shard_map/all_to_all | solution.py:10
  14.2 102.0 %all-gather.5.cloned.1.call-start = ((), (), s32[]{:S(2)}) async-start(), calls=%async_computation.6 | async-start | bytes 4718592 | tf_op jit(solution)/shard_map/all_gather | solution.py:81
  52.6 25.9 %copy-start = (bf16[1,4,8]{2,1,0:T(4,128)(2,1)S(1)}, bf16[1,4,8]{2,1,0:T(4,128)(2,1)}, u32[]{:S(2)}) copy-start(bf16[1,4,8]{2,1,0:T(4,128)(2,1)} %param.12) | copy-start | bytes 196
  67.0 94.8 %all-gather.3.cloned.1.call-start = ((), (), s32[]{:S(2)}) async-start(), calls=%async_computation.5 | async-start | bytes 4718592 | tf_op jit(solution)/shard_map/all_gather | solution.py:82
  203.2 5.0 %copy-start.1 = (u32[32]{0:T(128)S(1)}, u32[32]{0:T(128)}, u32[]{:S(2)}) copy-start(u32[32]{0:T(128)} %constant.65) | copy-start | bytes 388
  203.2 53.1 %all-to-all-start.4 = ((bf16[4,8,4,4,4096]{4,3,1,0,2:T(4,128)(2,1)}), bf16[4,8,4,4,4096]{4,3,1,0,2:T(4,128)(2,1)}, u32[]{:S(2)}, u32[]{:S(2)}) async-start(bf16[4,8,4,4,4096]{4,3,1,0,2:T(4,128)(2,1)} %copy.39), calls=%async_computation.4 | async-start | bytes 8388608 | tf_op jit(solution)/shard_map/all_to_all | solution.py:91
Sparse Core Ops, SparseCore 0:
  67.2 47.1 all-gather.4
  116.0 45.8 all-gather.2
